TPU v7x, 32 devices: a whole 2x2x4 slice. The times are simulated.
32 devices in a mesh: groups: 2 (over y), space: 4 (over z), ckpt: 2 (over x), rep: 2 (over core).
Axes of the slice: x: 2, y: 2, z: 4, core: 2. Of those that a mesh axis runs over, the one named last changes fastest.
Arguments:
- adj_disp: bfloat16 [320, 96, 768], P(('groups', 'space', 'rep'), None, 'ckpt'), parts along dimension 0, may hold values from -6 to 6
- adj_vel: bfloat16 [320, 96, 768], P(('groups', 'space', 'rep'), None, 'ckpt'), parts along dimension 0, may hold values from -6 to 6
- tangent_blocks: bfloat16 [320, 96, 768], P(('groups', 'space', 'rep')), parts along dimension 0, may hold values from -0.21875 to 0.21875
- block_cols: int32 [320, 8], P(('groups', 'space', 'rep')), parts along dimension 0, may hold values from 0 to 159, as said below
- inv_mass: float32 [320, 96], P(('groups', 'space', 'rep')), parts along dimension 0, may hold values from 0.25 to 1
- joint_stiff: float32 [320, 96], P(('groups', 'space', 'rep')), parts along dimension 0, may hold values from 0.2 to 1
- contact: int32 [3, 320], P(None, ('groups', 'space', 'rep')), parts along dimension 1, may hold values 0 or 1
- states: float32 [3, 320, 96], P(None, ('groups', 'space', 'rep'), 'ckpt'), parts along dimension 1, may hold values from -4 to 4
Outputs:
- disp_out: float32 [320, 96, 768], P(('groups', 'space', 'rep'), None, 'ckpt'), parts along dimension 0
- vel_out: float32 [320, 96, 768], P(('groups', 'space', 'rep'), None, 'ckpt'), parts along dimension 0
There are 2 independent parts, one for each index of `groups`. A program takes and returns all parts, laid end to end along the dimension named above; each array names one. Nothing has to cross between parts.
Inputs may be any that keep to these rules, and one draw needn't show every extreme that they name: `block_cols`: every block column lies within 4 block rows of its own block row, counted cyclically over the 160 block rows; each block row lists itself and the rows exactly 4 before and after it.
All inputs are finite; a program needn't handle non-finite values. No bound on the sum of `contact` on one device may be relied on, other than what follows from the above.
Results may differ from a plain program's by a relative error of at most 0.015.
Values may be sent and summed in bfloat16 or wider, within the bound.
No kernel may reach another device: no remote copies, remote signals or barrier semaphores. Data moves between devices by JAX's collectives and lax.ppermute only.
A program may use at most 128 MiB of HBM per device.

v0:
```python
import jax
import jax.numpy as jnp
from jax import lax
from jax.sharding import PartitionSpec as P

HB = 4
WINDOW = 3


def passed_along(array, axis, by):
    length = lax.axis_size(axis)
    return lax.ppermute(array, axis, [(i, (i + by) % length) for i in range(length)])


def body(adj_disp, adj_vel, tangent_blocks, block_cols, inv_mass, joint_stiff, contact, states):
    rows = tangent_blocks.shape[0]
    width = tangent_blocks.shape[1]
    slots = block_cols.shape[1]
    total_rows = rows * lax.axis_size(("space", "rep"))
    first = lax.axis_index(("space", "rep")) * rows
    local = jnp.arange(rows, dtype=jnp.int32)
    offset = jnp.mod(block_cols - (first + local)[:, None] + HB, total_rows) - HB
    position = local[:, None] + HB + offset
    disp = adj_disp.astype(jnp.float32)
    vel = adj_vel.astype(jnp.float32)
    accel = jnp.zeros(disp.shape, jnp.float32)
    for back in range(WINDOW):
        step = WINDOW - 1 - back
        state_now = lax.all_gather(states[step], "ckpt", axis=1, tiled=True)
        total = accel + 0.5 * vel
        packed = (inv_mass[:, :, None] * total).astype(jnp.bfloat16)
        coeff = (
            3.0 * joint_stiff * contact[step].astype(jnp.float32)[:, None] * state_now * state_now
        )
        lower = passed_along(packed[rows - HB :], ("space", "rep"), 1)
        upper = passed_along(packed[:HB], ("space", "rep"), -1)
        extended = jnp.concatenate([lower, packed, upper], axis=0)
        picked = extended[position].reshape(rows, slots * width, packed.shape[2])
        product = jnp.einsum(
            "bik,bkr->bir", tangent_blocks, picked, preferred_element_type=jnp.float32
        )
        image = product + coeff[:, :, None] * packed.astype(jnp.float32)
        disp = disp - image
        accel = 0.5 * disp + 0.5 * vel
        vel = vel + disp
    return (disp, vel)


def solution(mesh):
    placed = (
        P(("groups", "space", "rep"), None, "ckpt"),
        P(("groups", "space", "rep"), None, "ckpt"),
        P(("groups", "space", "rep"), None, None),
        P(("groups", "space", "rep"), None),
        P(("groups", "space", "rep"), None),
        P(("groups", "space", "rep"), None),
        P(None, ("groups", "space", "rep")),
        P(None, ("groups", "space", "rep"), "ckpt"),
    )
    return jax.shard_map(
        body,
        mesh=mesh,
        in_specs=placed,
        out_specs=(
            P(("groups", "space", "rep"), None, "ckpt"),
            P(("groups", "space", "rep"), None, "ckpt"),
        ),
        check_vma=False,
    )
```

profile of v0, /device:TPU:0, one launch (start us, length us, event | category | flops | bytes accessed | tf_op | source)
XLA Modules:
  0.0 129.3 jit_solution(14847695931026815950)
XLA Ops:
  0.6 0.0 copy-start
  0.6 0.0 copy-start.8
  0.7 0.9 broadcast_multiply_fusion
  1.5 1.7 %fusion = bf16[20,96,384]{2,1,0:T(8,128)(2,1)S(1)} fusion(bf16[20,96,384]{2,1,0:T(8,128)(2,1)} %param.9, f32[20,96]{1,0:T(8,128)S(1)} %broadcast_multiply_fusion), kind=kLoop, calls=%fused_computation.5 | loop fusion | flops 2211840 | bytes 2956800 | tf_op jit(solution)/shard_map/convert_element_type | solution.py:31
  3.3 0.0 copy-start.3
  3.3 1.1 copy-done.3
  4.4 0.9 fusion.10
  5.2 0.5 collective-permute-start
  5.7 4.0 %collective-permute-start.1 = (bf16[4,96,384]{2,1,0:T(8,128)(2,1)}, bf16[4,96,384]{2,1,0:T(8,128)(2,1)S(1)}, u32[]{:S(2)}, u32[]{:S(2)}) collective-permute-start(bf16[4,96,384]{2,1,0:T(8,128)(2,1)} %get-tuple-element.7), channel_id=1, source_target_pairs={{0,13},{1,0},{4,1},{5,4},{8,5},{9,8},{12,9},{13,12},{2,15},{3,2},{... | collective-permute-start | bytes 884744 | tf_op jit(solution)/shard_map/ppermute | solution.py:12
  9.7 0.0 copy-done.8
  9.7 0.6 multiply_bitcast_fusion
  10.3 0.7 compare_select_fusion
  11.1 0.7 copy.21
  11.7 1.4 %reshape.55 = s32[160]{0:T(256)} reshape(s32[20,8]{1,0:T(8,128)} %copy.21) | data formatting | bytes 1280 | tf_op jit(solution)/shard_map/broadcast_in_dim | solution.py:38
  13.1 1.4 %fusion.11 = (f32[1,20,48]{2,1,0:T(8,128)}, f32[1,20,48]{2,1,0:T(8,128)}, f32[1,20,48]{2,1,0:T(8,128)}) fusion(f32[3,20,48]{2,1,0:T(8,128)} %param.15), kind=kLoop, calls=%fused_computation.37 | loop fusion | bytes 23040 | tf_op jit(solution)/shard_map/slice | solution.py:29
  14.5 1.4 %copy.30 = f32[1,20,48]{1,0,2:T(1,128)} copy(f32[1,20,48]{2,1,0:T(8,128)} %get-tuple-element.8) | data formatting | bytes 7680
  15.9 6.1 %all-gather.2 = f32[1,20,96]{1,0,2:T(1,128)} all-gather(f32[1,20,48]{1,0,2:T(1,128)} %copy.30), channel_id=4, replica_groups=mesh['groups'=2,'space'=4,'ckpt'=2,'rep'=2] {'ckpt'}, dimensions={2}, use_global_device_ids=true | all-gather | bytes 11520 | tf_op jit(solution)/shard_map/all_gather | solution.py:29
  21.9 1.5 %copy.27 = f32[1,20,96]{2,1,0:T(8,128)} copy(f32[1,20,96]{1,0,2:T(1,128)} %all-gather.2) | data formatting | bytes 15360 | tf_op jit(solution)/shard_map/all_gather | solution.py:29
  23.4 1.4 %copy.29 = f32[1,20,48]{1,0,2:T(1,128)} copy(f32[1,20,48]{2,1,0:T(8,128)} %get-tuple-element.9) | data formatting | bytes 7680
  24.8 4.8 %all-gather.1 = f32[1,20,96]{1,0,2:T(1,128)} all-gather(f32[1,20,48]{1,0,2:T(1,128)} %copy.29), channel_id=3, replica_groups=mesh['groups'=2,'space'=4,'ckpt'=2,'rep'=2] {'ckpt'}, dimensions={2}, use_global_device_ids=true | all-gather | bytes 11520 | tf_op jit(solution)/shard_map/all_gather | solution.py:29
  29.6 1.5 %copy.25 = f32[1,20,96]{2,1,0:T(8,128)} copy(f32[1,20,96]{1,0,2:T(1,128)} %all-gather.1) | data formatting | bytes 15360 | tf_op jit(solution)/shard_map/all_gather | solution.py:29
  31.1 1.4 %copy.28 = f32[1,20,48]{1,0,2:T(1,128)} copy(f32[1,20,48]{2,1,0:T(8,128)} %get-tuple-element.10) | data formatting | bytes 7680
  32.5 5.4 %all-gather = f32[1,20,96]{1,0,2:T(1,128)} all-gather(f32[1,20,48]{1,0,2:T(1,128)} %copy.28), channel_id=2, replica_groups=mesh['groups'=2,'space'=4,'ckpt'=2,'rep'=2] {'ckpt'}, dimensions={2}, use_global_device_ids=true | all-gather | bytes 11520 | tf_op jit(solution)/shard_map/all_gather | solution.py:29
  37.9 1.5 %copy.23 = f32[1,20,96]{2,1,0:T(8,128)} copy(f32[1,20,96]{1,0,2:T(1,128)} %all-gather) | data formatting | bytes 15360 | tf_op jit(solution)/shard_map/all_gather | solution.py:29
  39.4 0.7 pad_clamp_fusion
  40.0 1.5 %multiply_multiply_fusion = (f32[20,96]{1,0:T(8,128)}, f32[20,96]{1,0:T(8,128)}, f32[20,96]{1,0:T(8,128)}) fusion(f32[1,20,96]{2,1,0:T(8,128)} %copy.27, f32[20,96]{1,0:T(8,128)} %param.13, f32[20]{0:T(128)} %get-tuple-element.14, f32[1,20,96]{2,1,0:T(8,128)} %copy.23, f32[20]{0:T(128)} %get-tuple-element.15, f32[1,20,96]{2,1,0:T(8,128)} %copy.25, ...), kind=kLoop, calls=%fused_computation.19 | loop fusion | flops 17280 | bytes 54000 | tf_op jit(solution)/shard_map/mul | solution.py:33
  41.5 0.0 collective-permute-done
  41.5 0.0 collective-permute-done.1
  41.5 3.0 %pad_maximum_fusion = bf16[28,96,384]{2,1,0:T(8,128)(2,1)} fusion(bf16[4,96,384]{2,1,0:T(8,128)(2,1)S(1)} %collective-permute-done.1, bf16[20,96,384]{2,1,0:T(8,128)(2,1)} %copy-done.3, bf16[4,96,384]{2,1,0:T(8,128)(2,1)S(1)} %collective-permute-done), kind=kLoop, calls=%fused_computation.14 | loop fusion | flops 2064384 | bytes 4128768 | tf_op jit(solution)/shard_map/concatenate | solution.py:37
  44.5 0.0 copy-start.4
  44.5 0.0 copy-start.6
  44.5 10.3 %gather_fusion = bf16[160,96,384]{2,1,0:T(8,128)(2,1)} fusion(bf16[28,96,384]{2,1,0:T(8,128)(2,1)} %pad_maximum_fusion, s32[1024]{0:T(1024)S(1)} %pad_clamp_fusion), kind=kCustom, calls=%fused_computation | custom fusion | bytes 23593600 | tf_op jit(solution)/shard_map/gather | solution.py:38
  54.8 0.0 copy-done
  54.8 0.0 copy-done.4
  54.8 0.0 copy-done.6
  54.8 7.6 %multiply_convert_fusion.1 = (bf16[20,96,384]{2,1,0:T(8,128)(2,1)S(1)}, f32[20,96,384]{2,1,0:T(8,128)}) fusion(f32[20,96]{1,0:T(8,128)S(1)} %copy-done.4, bf16[20,96,384]{2,1,0:T(8,128)(2,1)} %param.9, f32[20,96]{1,0:T(8,128)S(1)} %copy-done.6, bf16[20,96,768]{2,1,0:T(8,128)(2,1)S(1)} %copy-done, bf16[20,768,384]{2,1,0:T(8,128)(2,1)} %bitcast.34, ...), kind=kOutput, calls=%fused_computation.13 | convolution fusion | flops 1142046720 | bytes 22141440 | tf_op jit(solution)/shard_map/bik,bkr->bir/dot_general | solution.py:39
  62.3 0.0 copy-start.1
  62.3 0.1 fusion.9
  62.4 0.1 collective-permute-start.2
  62.5 3.5 %collective-permute-start.3 = (bf16[4,96,384]{2,1,0:T(8,128)(2,1)S(1)}, bf16[4,96,384]{2,1,0:T(8,128)(2,1)S(1)}, u32[]{:S(2)}, u32[]{:S(2)}) collective-permute-start(bf16[4,96,384]{2,1,0:T(8,128)(2,1)S(1)} %get-tuple-element.5), channel_id=1, source_target_pairs={{0,13},{1,0},{4,1},{5,4},{8,5},{9,8},{12,9},{13,12},{2,15},{3,2},{... | collective-permute-start | bytes 884744 | tf_op jit(solution)/shard_map/ppermute | solution.py:12
  66.0 7.3 %collective-permute-done.2 = bf16[4,96,384]{2,1,0:T(8,128)(2,1)S(1)} collective-permute-done((bf16[4,96,384]{2,1,0:T(8,128)(2,1)S(1)}, bf16[4,96,384]{2,1,0:T(8,128)(2,1)S(1)}, u32[]{:S(2)}, u32[]{:S(2)}) %collective-permute-start.2) | collective-permute-done | bytes 294944 | tf_op jit(solution)/shard_map/ppermute | solution.py:12
  73.3 0.0 collective-permute-done.3
  73.3 0.0 copy-done.1
  73.3 1.6 %pad_maximum_fusion.1 = bf16[28,96,384]{2,1,0:T(8,128)(2,1)} fusion(bf16[4,96,384]{2,1,0:T(8,128)(2,1)S(1)} %collective-permute-done.3, bf16[20,96,384]{2,1,0:T(8,128)(2,1)S(1)} %get-tuple-element.17, bf16[4,96,384]{2,1,0:T(8,128)(2,1)S(1)} %collective-permute-done.2), kind=kLoop, calls=%fused_computation.15 | loop fusion | flops 2064384 | bytes 4128768 | tf_op jit(solution)/shard_map/concatenate | solution.py:37
  74.9 0.0 copy-start.5
  74.9 10.3 %gather_fusion.1 = bf16[160,96,384]{2,1,0:T(8,128)(2,1)} fusion(bf16[28,96,384]{2,1,0:T(8,128)(2,1)} %pad_maximum_fusion.1, s32[1024]{0:T(1024)S(1)} %pad_clamp_fusion), kind=kCustom, calls=%fused_computation.1 | custom fusion | bytes 23593600 | tf_op jit(solution)/shard_map/gather | solution.py:38
  85.2 0.0 copy-done.5
  85.2 10.4 %multiply_convert_fusion = (bf16[20,96,384]{2,1,0:T(8,128)(2,1)S(1)}, f32[20,96,384]{2,1,0:T(8,128)}) fusion(f32[20,96]{1,0:T(8,128)S(1)} %copy-done.4, f32[20,96,384]{2,1,0:T(8,128)} %get-tuple-element.18, bf16[20,96,384]{2,1,0:T(8,128)(2,1)} %param.9, bf16[20,96,384]{2,1,0:T(8,128)(2,1)} %copy-done.1, f32[20,96]{1,0:T(8,128)S(1)} %copy-done.5, ...), kind=kOutput, calls=%fused_computation.12 | convolution fusion | flops 1142784000 | bytes 25082880 | tf_op jit(solution)/shard_map/bik,bkr->bir/dot_general | solution.py:39
  95.6 0.0 copy-start.2
  95.6 0.1 fusion.8
  95.6 0.1 collective-permute-start.4
  95.7 3.5 %collective-permute-start.5 = (bf16[4,96,384]{2,1,0:T(8,128)(2,1)S(1)}, bf16[4,96,384]{2,1,0:T(8,128)(2,1)S(1)}, u32[]{:S(2)}, u32[]{:S(2)}) collective-permute-start(bf16[4,96,384]{2,1,0:T(8,128)(2,1)S(1)} %get-tuple-element.3), channel_id=1, source_target_pairs={{0,13},{1,0},{4,1},{5,4},{8,5},{9,8},{12,9},{13,12},{2,15},{3,2},{... | collective-permute-start | bytes 884744 | tf_op jit(solution)/shard_map/ppermute | solution.py:12
  99.2 6.3 %collective-permute-done.4 = bf16[4,96,384]{2,1,0:T(8,128)(2,1)S(1)} collective-permute-done((bf16[4,96,384]{2,1,0:T(8,128)(2,1)S(1)}, bf16[4,96,384]{2,1,0:T(8,128)(2,1)S(1)}, u32[]{:S(2)}, u32[]{:S(2)}) %collective-permute-start.4) | collective-permute-done | bytes 294944 | tf_op jit(solution)/shard_map/ppermute | solution.py:12
  105.5 0.0 collective-permute-done.5
  105.5 0.0 copy-done.2
  105.5 1.7 %pad_maximum_fusion.2 = bf16[28,96,384]{2,1,0:T(8,128)(2,1)} fusion(bf16[4,96,384]{2,1,0:T(8,128)(2,1)S(1)} %collective-permute-done.5, bf16[20,96,384]{2,1,0:T(8,128)(2,1)S(1)} %get-tuple-element.19, bf16[4,96,384]{2,1,0:T(8,128)(2,1)S(1)} %collective-permute-done.4), kind=kLoop, calls=%fused_computation.16 | loop fusion | flops 2064384 | bytes 4128768 | tf_op jit(solution)/shard_map/concatenate | solution.py:37
  107.2 0.0 copy-start.7
  107.2 10.3 %gather_fusion.2 = bf16[160,96,384]{2,1,0:T(8,128)(2,1)} fusion(bf16[28,96,384]{2,1,0:T(8,128)(2,1)} %pad_maximum_fusion.2, s32[1024]{0:T(1024)S(1)} %pad_clamp_fusion), kind=kCustom, calls=%fused_computation.2 | custom fusion | bytes 23593600 | tf_op jit(solution)/shard_map/gather | solution.py:38
  117.5 0.0 copy-done.7
  117.5 11.8 %fusion.5 = (f32[20,96,384]{2,1,0:T(8,128)}, f32[20,96,384]{2,1,0:T(8,128)}) fusion(f32[20,96,384]{2,1,0:T(8,128)} %get-tuple-element.20, f32[20,96,384]{2,1,0:T(8,128)} %get-tuple-element.18, bf16[20,96,384]{2,1,0:T(8,128)(2,1)} %param.9, bf16[20,96,384]{2,1,0:T(8,128)(2,1)} %copy-done.2, f32[20,96]{1,0:T(8,128)S(1)} %copy-done.7, ...), kind=kOutput, calls=%fused_computation.18 | convolution fusion | flops 1138360320 | bytes 29498880 | tf_op jit(solution)/shard_map/bik,bkr->bir/dot_general | solution.py:39
  (1 shorter events, 0.0 us)
Async XLA Ops:
  0.6 54.2 %copy-start = (bf16[20,96,768]{2,1,0:T(8,128)(2,1)S(1)}, bf16[20,96,768]{2,1,0:T(8,128)(2,1)}, u32[]{:S(2)}) copy-start(bf16[20,96,768]{2,1,0:T(8,128)(2,1)} %param.10) | copy-start | bytes 8847364
  0.6 9.1 %copy-start.8 = (s32[3,20]{1,0:T(4,128)S(1)}, s32[3,20]{1,0:T(4,128)}, u32[]{:S(2)}) copy-start(s32[3,20]{1,0:T(4,128)} %param.14) | copy-start | bytes 724
  3.3 1.1 copy-start.3
  5.2 36.2 %collective-permute-start = (bf16[4,96,384]{2,1,0:T(8,128)(2,1)}, bf16[4,96,384]{2,1,0:T(8,128)(2,1)S(1)}, u32[]{:S(2)}, u32[]{:S(2)}) collective-permute-start(bf16[4,96,384]{2,1,0:T(8,128)(2,1)} %get-tuple-element.6), channel_id=1, source_target_pairs={{0,1},{1,4},{4,5},{5,8},{8,9},{9,12},{12,13},{13,0},{2,3},{3,6},{6... | collective-permute-start | bytes 884744 | tf_op jit(solution)/shard_map/ppermute | solution.py:12
  5.7 35.8 %collective-permute-start.1 = (bf16[4,96,384]{2,1,0:T(8,128)(2,1)}, bf16[4,96,384]{2,1,0:T(8,128)(2,1)S(1)}, u32[]{:S(2)}, u32[]{:S(2)}) collective-permute-start(bf16[4,96,384]{2,1,0:T(8,128)(2,1)} %get-tuple-element.7), channel_id=1, source_target_pairs={{0,13},{1,0},{4,1},{5,4},{8,5},{9,8},{12,9},{13,12},{2,15},{3,2},{... | collective-permute-start | bytes 884744 | tf_op jit(solution)/shard_map/ppermute | solution.py:12
  44.5 10.3 %copy-start.4 = (f32[20,96]{1,0:T(8,128)S(1)}, f32[20,96]{1,0:T(8,128)}, u32[]{:S(2)}) copy-start(f32[20,96]{1,0:T(8,128)} %param.12) | copy-start | bytes 23044
  44.5 10.3 %copy-start.6 = (f32[20,96]{1,0:T(8,128)S(1)}, f32[20,96]{1,0:T(8,128)}, u32[]{:S(2)}) copy-start(f32[20,96]{1,0:T(8,128)} %get-tuple-element.12) | copy-start | bytes 23044
  62.3 10.9 %copy-start.1 = (bf16[20,96,384]{2,1,0:T(8,128)(2,1)}, bf16[20,96,384]{2,1,0:T(8,128)(2,1)S(1)}, u32[]{:S(2)}) copy-start(bf16[20,96,384]{2,1,0:T(8,128)(2,1)S(1)} %get-tuple-element.17) | copy-start | bytes 4423684
  62.4 10.9 %collective-permute-start.2 = (bf16[4,96,384]{2,1,0:T(8,128)(2,1)S(1)}, bf16[4,96,384]{2,1,0:T(8,128)(2,1)S(1)}, u32[]{:S(2)}, u32[]{:S(2)}) collective-permute-start(bf16[4,96,384]{2,1,0:T(8,128)(2,1)S(1)} %get-tuple-element.4), channel_id=1, source_target_pairs={{0,1},{1,4},{4,5},{5,8},{8,9},{9,12},{12,13},{13,0},{2,3},{3,6},{6... | collective-permute-start | bytes 884744 | tf_op jit(solution)/shard_map/ppermute | solution.py:12
  62.5 10.8 %collective-permute-start.3 = (bf16[4,96,384]{2,1,0:T(8,128)(2,1)S(1)}, bf16[4,96,384]{2,1,0:T(8,128)(2,1)S(1)}, u32[]{:S(2)}, u32[]{:S(2)}) collective-permute-start(bf16[4,96,384]{2,1,0:T(8,128)(2,1)S(1)} %get-tuple-element.5), channel_id=1, source_target_pairs={{0,13},{1,0},{4,1},{5,4},{8,5},{9,8},{12,9},{13,12},{2,15},{3,2},{... | collective-permute-start | bytes 884744 | tf_op jit(solution)/shard_map/ppermute | solution.py:12
  74.9 10.3 %copy-start.5 = (f32[20,96]{1,0:T(8,128)S(1)}, f32[20,96]{1,0:T(8,128)}, u32[]{:S(2)}) copy-start(f32[20,96]{1,0:T(8,128)} %get-tuple-element.13) | copy-start | bytes 23044
  95.6 10.0 %copy-start.2 = (bf16[20,96,384]{2,1,0:T(8,128)(2,1)}, bf16[20,96,384]{2,1,0:T(8,128)(2,1)S(1)}, u32[]{:S(2)}) copy-start(bf16[20,96,384]{2,1,0:T(8,128)(2,1)S(1)} %get-tuple-element.19) | copy-start | bytes 4423684
  95.6 9.9 %collective-permute-start.4 = (bf16[4,96,384]{2,1,0:T(8,128)(2,1)S(1)}, bf16[4,96,384]{2,1,0:T(8,128)(2,1)S(1)}, u32[]{:S(2)}, u32[]{:S(2)}) collective-permute-start(bf16[4,96,384]{2,1,0:T(8,128)(2,1)S(1)} %get-tuple-element.2), channel_id=1, source_target_pairs={{0,1},{1,4},{4,5},{5,8},{8,9},{9,12},{12,13},{13,0},{2,3},{3,6},{6... | collective-permute-start | bytes 884744 | tf_op jit(solution)/shard_map/ppermute | solution.py:12
  95.7 9.8 %collective-permute-start.5 = (bf16[4,96,384]{2,1,0:T(8,128)(2,1)S(1)}, bf16[4,96,384]{2,1,0:T(8,128)(2,1)S(1)}, u32[]{:S(2)}, u32[]{:S(2)}) collective-permute-start(bf16[4,96,384]{2,1,0:T(8,128)(2,1)S(1)} %get-tuple-element.3), channel_id=1, source_target_pairs={{0,13},{1,0},{4,1},{5,4},{8,5},{9,8},{12,9},{13,12},{2,15},{3,2},{... | collective-permute-start | bytes 884744 | tf_op jit(solution)/shard_map/ppermute | solution.py:12
  107.2 10.3 %copy-start.7 = (f32[20,96]{1,0:T(8,128)S(1)}, f32[20,96]{1,0:T(8,128)}, u32[]{:S(2)}) copy-start(f32[20,96]{1,0:T(8,128)} %get-tuple-element.11) | copy-start | bytes 23044
where the time goes:
time: 130 us; the launch traced here: 129 us
  local copies, waits for them, and re-layouts  45 us (35%)
  matrix products  29.8 us (23%)
  blocking collectives  16.3 us (13%)
  waiting for transfers between devices  13.6 us (10%)
  other arithmetic  12.3 us (9%)
  starting transfers between devices  11.7 us (9%)
    gather x3, local copies, waits for them, and re-layouts, body(): picked = extended[position].reshape(rows, slots * width, packed.shape[2])  30.9 us
    dot_general x3, matrix products, body(): jnp.einsum('bik,bkr->bir', tangent_blocks, picked, preferred_element_type...  29.8 us
    all_gather x3, blocking collectives, body(): state_now = lax.all_gather(states[step], 'ckpt', axis=1, tiled=True)  16.3 us
    ppermute x6, waiting for transfers between devices, passed_along(): lax.ppermute(array, axis, [(i, (i + by) % length) for i in range(length)])  13.6 us
    ppermute x6, starting transfers between devices, passed_along(): lax.ppermute(array, axis, [(i, (i + by) % length) for i in range(length)])  11.7 us
    concatenate x3, other arithmetic, body(): extended = jnp.concatenate([lower, packed, upper], axis=0)  6.24 us
    unnamed x21, local copies, waits for them, and re-layouts  5.3 us
    all_gather x3, local copies, waits for them, and re-layouts, body(): state_now = lax.all_gather(states[step], 'ckpt', axis=1, tiled=True)  4.42 us
  transfers between devices with their start and end apart: 6, of which 2 were waited for; matrix products, arithmetic and copies ran while one was open for 12% of the time, Pallas kernels for 0%

commit v1 on v0

--- a/solution.py
+++ b/solution.py
@@ -5,6 +5,27 @@
 
 HB = 4
 WINDOW = 3
+
+
+def joined_along(blocks, dim):
+    blocks = jnp.moveaxis(blocks, 0, dim)
+    lengths = blocks.shape
+    return blocks.reshape(*lengths[:dim], lengths[dim] * lengths[dim + 1], *lengths[dim + 2 :])
+
+
+def grow_blocks(x, axis):
+    size, position = (lax.axis_size(axis), lax.axis_index(axis))
+    blocks, bit = (x[None], 1)
+    while bit < size:
+        other = lax.ppermute(blocks, axis, [(i, i ^ bit) for i in range(size)])
+        low = position & bit == 0
+        blocks = jnp.concatenate([jnp.where(low, blocks, other), jnp.where(low, other, blocks)])
+        bit *= 2
+    return blocks
+
+
+def gather_by_bits(shard, axis, dim):
+    return joined_along(grow_blocks(shard, axis), dim)
 
 
 def passed_along(array, axis, by):
@@ -26,7 +47,7 @@
     accel = jnp.zeros(disp.shape, jnp.float32)
     for back in range(WINDOW):
         step = WINDOW - 1 - back
-        state_now = lax.all_gather(states[step], "ckpt", axis=1, tiled=True)
+        state_now = gather_by_bits(states[step], "ckpt", 1)
         total = accel + 0.5 * vel
         packed = (inv_mass[:, :, None] * total).astype(jnp.bfloat16)
         coeff = (

time: 130 us -> 119 us (0.915)
  blocking collectives: 16.3 us -> 0 us
  starting transfers between devices: 11.7 us -> 15.7 us
  other arithmetic: 12.3 us -> 14.8 us
  local copies, waits for them, and re-layouts: 45 us -> 43.2 us
    all_gather x3 -> x0, blocking collectives: 16.3 us -> none  [body(): state_now = lax.all_gather(states[step], 'ckpt', axis=1, tiled=True)]
    ppermute x0 -> x3, starting transfers between devices: none -> 4.96 us  [grow_blocks(): other = lax.ppermute(blocks, axis, [(i, i ^ bit) for i in range(size)])]
    all_gather x3 -> x0, local copies, waits for them, and re-layouts: 4.42 us -> none  [body(): state_now = lax.all_gather(states[step], 'ckpt', axis=1, tiled=True)]
    reshape x0 -> x3, local copies, waits for them, and re-layouts: none -> 4.21 us  [joined_along(): blocks.reshape(*lengths[:dim], lengths[dim] * lengths[dim + 1], *lengths[...]
    unnamed x21 -> x18, local copies, waits for them, and re-layouts: 5.3 us -> 1.14 us
    transpose x0 -> x3, local copies, waits for them, and re-layouts: none -> 2.56 us  [joined_along(): blocks = jnp.moveaxis(blocks, 0, dim)]
    select_n x0 -> x2, other arithmetic: none -> 2.12 us  [grow_blocks(): jnp.where(low, blocks, other)]
  transfers between devices with their start and end apart: 6 -> 9, of which waited for: 2 -> 3; matrix products, arithmetic and copies ran while one was open for 12% -> 15% of each run, Pallas kernels for 0% -> 0%
where the time goes in v1:
time: 119 us; the launch traced here: 118 us
  local copies, waits for them, and re-layouts  43.2 us (36%)
  matrix products  29.8 us (25%)
  starting transfers between devices  15.7 us (13%)
  other arithmetic  14.8 us (12%)
  waiting for transfers between devices  13.7 us (12%)
    gather x3, local copies, waits for them, and re-layouts, body(): picked = extended[position].reshape(rows, slots * width, packed.shape[2])  30.8 us
    dot_general x3, matrix products, body(): jnp.einsum('bik,bkr->bir', tangent_blocks, picked, preferred_element_type...  29.8 us
    ppermute x6, waiting for transfers between devices, passed_along(): lax.ppermute(array, axis, [(i, (i + by) % length) for i in range(length)])  13.6 us
    ppermute x6, starting transfers between devices, passed_along(): lax.ppermute(array, axis, [(i, (i + by) % length) for i in range(length)])  10.7 us
    concatenate x3, other arithmetic, body(): extended = jnp.concatenate([lower, packed, upper], axis=0)  6.22 us
    ppermute x3, starting transfers between devices, grow_blocks(): other = lax.ppermute(blocks, axis, [(i, i ^ bit) for i in range(size)])  4.96 us
    reshape x3, local copies, waits for them, and re-layouts, joined_along(): blocks.reshape(*lengths[:dim], lengths[dim] * lengths[dim + 1], *lengths[...  4.21 us
    transpose x3, local copies, waits for them, and re-layouts, joined_along(): blocks = jnp.moveaxis(blocks, 0, dim)  2.56 us
  transfers between devices with their start and end apart: 9, of which 3 were waited for; matrix products, arithmetic and copies ran while one was open for 15% of the time, Pallas kernels for 0%

profile of v1, /device:TPU:0, one launch (start us, length us, event | category | flops | bytes accessed | tf_op | source)
XLA Modules:
  0.0 117.9 jit_solution(3998810670776794092)
XLA Ops:
  0.6 0.0 copy-start
  0.6 0.0 copy-start.8
  0.7 1.5 %slice.47 = f32[1,20,48]{2,1,0:T(8,128)} slice(f32[3,20,48]{2,1,0:T(8,128)} %param.15), slice={[0:1], [0:20], [0:48]} | slice | bytes 7680 | tf_op jit(solution)/shard_map/slice | solution.py:50
  2.1 2.9 %collective-permute-start.8 = (f32[1,20,48]{2,1,0:T(8,128)}, f32[1,20,48]{2,1,0:T(8,128)}, u32[]{:S(2)}, u32[]{:S(2)}) collective-permute-start(f32[1,20,48]{2,1,0:T(8,128)} %slice.47), channel_id=1, source_target_pairs={{0,2},{2,0},{1,3},{3,1},{4,6},{6,4},{5,7},{7,5},{8,10},{10,8},{9,1... | collective-permute-start | bytes 11528 | tf_op jit(solution)/shard_map/ppermute | solution.py:20
  5.1 0.7 broadcast_multiply_fusion
  5.8 1.7 %fusion = bf16[20,96,384]{2,1,0:T(8,128)(2,1)S(1)} fusion(bf16[20,96,384]{2,1,0:T(8,128)(2,1)} %param.9, f32[20,96]{1,0:T(8,128)S(1)} %broadcast_multiply_fusion), kind=kLoop, calls=%fused_computation.5 | loop fusion | flops 2211840 | bytes 2956800 | tf_op jit(solution)/shard_map/convert_element_type | solution.py:52
  7.5 0.0 copy-start.3
  7.5 1.1 copy-done.3
  8.6 0.9 fusion.10
  9.5 0.0 collective-permute-start
  9.5 3.5 %collective-permute-start.1 = (bf16[4,96,384]{2,1,0:T(8,128)(2,1)}, bf16[4,96,384]{2,1,0:T(8,128)(2,1)S(1)}, u32[]{:S(2)}, u32[]{:S(2)}) collective-permute-start(bf16[4,96,384]{2,1,0:T(8,128)(2,1)} %get-tuple-element.7), channel_id=1, source_target_pairs={{0,13},{1,0},{4,1},{5,4},{8,5},{9,8},{12,9},{13,12},{2,15},{3,2},{... | collective-permute-start | bytes 884744 | tf_op jit(solution)/shard_map/ppermute | solution.py:33
  13.0 0.0 copy-done.8
  13.0 0.6 multiply_bitcast_fusion
  13.6 0.7 compare_select_fusion
  14.3 0.7 copy.10
  15.0 1.4 %reshape.67 = s32[160]{0:T(256)} reshape(s32[20,8]{1,0:T(8,128)} %copy.10) | data formatting | bytes 1280 | tf_op jit(solution)/shard_map/broadcast_in_dim | solution.py:59
  16.3 0.7 pad_clamp_fusion
  17.0 0.0 collective-permute-done.8
  17.0 1.4 %broadcast_select_fusion.1 = (f32[1,20,48]{2,1,0:T(8,128)S(1)}, f32[1,20,48]{2,1,0:T(8,128)S(1)}, f32[1,20,48]{2,1,0:T(8,128)}, f32[1,20,48]{2,1,0:T(8,128)}) fusion(f32[1,20,48]{2,1,0:T(8,128)} %collective-permute-done.8, pred[]{:T(512)S(6)} %eq.4, f32[3,20,48]{2,1,0:T(8,128)} %param.15), kind=kLoop, calls=%fused_computation.29 | loop fusion | flops 1920 | bytes 30721 | tf_op jit(solution)/shard_map/jit(_where)/select_n | solution.py:22
  18.4 0.0 collective-permute-start.2
  18.4 2.0 %collective-permute-start.5 = (f32[1,20,48]{2,1,0:T(8,128)}, f32[1,20,48]{2,1,0:T(8,128)}, u32[]{:S(2)}, u32[]{:S(2)}) collective-permute-start(f32[1,20,48]{2,1,0:T(8,128)} %get-tuple-element.15), channel_id=1, source_target_pairs={{0,2},{2,0},{1,3},{3,1},{4,6},{6,4},{5,7},{7,5},{8,10},{10,8},{9,1... | collective-permute-start | bytes 11528 | tf_op jit(solution)/shard_map/ppermute | solution.py:20
  20.4 0.6 copy.13
  21.0 1.4 %reshape.64 = f32[20,96]{1,0:T(8,128)} reshape(f32[20,2,48]{2,1,0:T(2,128)} %copy.13) | data formatting | bytes 15360 | tf_op jit(solution)/shard_map/reshape | solution.py:13
  22.4 0.0 collective-permute-done.2
  22.4 0.1 collective-permute-done.5
  22.5 0.8 broadcast_select_fusion.3
  23.3 0.6 maximum_bitcast_fusion
  23.9 0.6 copy.11
  24.5 1.4 %reshape.60 = f32[20,96]{1,0:T(8,128)} reshape(f32[20,2,48]{2,1,0:T(2,128)} %copy.11) | data formatting | bytes 15360 | tf_op jit(solution)/shard_map/reshape | solution.py:13
  25.9 1.3 %copy.12 = f32[20,2,48]{2,1,0:T(2,128)} copy(f32[20,2,48]{2,0,1:T(8,128)} %get-tuple-element.31) | data formatting | bytes 15360 | tf_op jit(solution)/shard_map/transpose | solution.py:11
  27.2 1.4 %reshape.62 = f32[20,96]{1,0:T(8,128)} reshape(f32[20,2,48]{2,1,0:T(2,128)} %copy.12) | data formatting | bytes 15360 | tf_op jit(solution)/shard_map/reshape | solution.py:13
  28.7 1.4 %multiply_multiply_fusion = (f32[20,96]{1,0:T(8,128)}, f32[20,96]{1,0:T(8,128)}, f32[20,96]{1,0:T(8,128)}) fusion(f32[20,96]{1,0:T(8,128)} %reshape.64, f32[20,96]{1,0:T(8,128)} %param.13, f32[20]{0:T(128)} %get-tuple-element.21, f32[20,96]{1,0:T(8,128)} %reshape.60, f32[20]{0:T(128)} %get-tuple-element.22, f32[20,96]{1,0:T(8,128)} %reshape.62, ...), kind=kLoop, calls=%fused_computation.22 | loop fusion | flops 17280 | bytes 54000 | tf_op jit(solution)/shard_map/mul | solution.py:54
  30.1 0.0 collective-permute-done
  30.1 0.0 collective-permute-done.1
  30.1 3.0 %pad_maximum_fusion = bf16[28,96,384]{2,1,0:T(8,128)(2,1)} fusion(bf16[4,96,384]{2,1,0:T(8,128)(2,1)S(1)} %collective-permute-done.1, bf16[20,96,384]{2,1,0:T(8,128)(2,1)} %copy-done.3, bf16[4,96,384]{2,1,0:T(8,128)(2,1)S(1)} %collective-permute-done), kind=kLoop, calls=%fused_computation.14 | loop fusion | flops 2064384 | bytes 4128768 | tf_op jit(solution)/shard_map/concatenate | solution.py:58
  33.1 0.0 copy-start.4
  33.1 10.3 %gather_fusion = bf16[160,96,384]{2,1,0:T(8,128)(2,1)} fusion(bf16[28,96,384]{2,1,0:T(8,128)(2,1)} %pad_maximum_fusion, s32[1024]{0:T(1024)S(1)} %pad_clamp_fusion), kind=kCustom, calls=%fused_computation | custom fusion | bytes 23593600 | tf_op jit(solution)/shard_map/gather | solution.py:59
  43.4 0.0 copy-done
  43.4 0.0 copy-done.4
  43.4 0.0 copy-done.6
  43.4 7.6 %multiply_convert_fusion.1 = (bf16[20,96,384]{2,1,0:T(8,128)(2,1)S(1)}, f32[20,96,384]{2,1,0:T(8,128)}) fusion(f32[20,96]{1,0:T(8,128)S(1)} %copy-done.4, bf16[20,96,384]{2,1,0:T(8,128)(2,1)} %param.9, f32[20,96]{1,0:T(8,128)S(1)} %copy-done.6, bf16[20,96,768]{2,1,0:T(8,128)(2,1)S(1)} %copy-done, bf16[20,768,384]{2,1,0:T(8,128)(2,1)} %bitcast.34, ...), kind=kOutput, calls=%fused_computation.13 | convolution fusion | flops 1142046720 | bytes 22141440 | tf_op jit(solution)/shard_map/bik,bkr->bir/dot_general | solution.py:60
  50.9 0.0 copy-start.1
  50.9 0.1 fusion.9
  51.0 0.1 collective-permute-start.3
  51.1 3.5 %collective-permute-start.4 = (bf16[4,96,384]{2,1,0:T(8,128)(2,1)S(1)}, bf16[4,96,384]{2,1,0:T(8,128)(2,1)S(1)}, u32[]{:S(2)}, u32[]{:S(2)}) collective-permute-start(bf16[4,96,384]{2,1,0:T(8,128)(2,1)S(1)} %get-tuple-element.5), channel_id=1, source_target_pairs={{0,13},{1,0},{4,1},{5,4},{8,5},{9,8},{12,9},{13,12},{2,15},{3,2},{... | collective-permute-start | bytes 884744 | tf_op jit(solution)/shard_map/ppermute | solution.py:33
  54.6 6.9 %collective-permute-done.3 = bf16[4,96,384]{2,1,0:T(8,128)(2,1)S(1)} collective-permute-done((bf16[4,96,384]{2,1,0:T(8,128)(2,1)S(1)}, bf16[4,96,384]{2,1,0:T(8,128)(2,1)S(1)}, u32[]{:S(2)}, u32[]{:S(2)}) %collective-permute-start.3) | collective-permute-done | bytes 294944 | tf_op jit(solution)/shard_map/ppermute | solution.py:33
  61.5 0.0 collective-permute-done.4
  61.5 0.0 copy-done.1
  61.5 1.6 %pad_maximum_fusion.1 = bf16[28,96,384]{2,1,0:T(8,128)(2,1)} fusion(bf16[4,96,384]{2,1,0:T(8,128)(2,1)S(1)} %collective-permute-done.4, bf16[20,96,384]{2,1,0:T(8,128)(2,1)S(1)} %get-tuple-element.24, bf16[4,96,384]{2,1,0:T(8,128)(2,1)S(1)} %collective-permute-done.3), kind=kLoop, calls=%fused_computation.15 | loop fusion | flops 2064384 | bytes 4128768 | tf_op jit(solution)/shard_map/concatenate | solution.py:58
  63.1 0.0 copy-start.5
  63.1 10.3 %gather_fusion.1 = bf16[160,96,384]{2,1,0:T(8,128)(2,1)} fusion(bf16[28,96,384]{2,1,0:T(8,128)(2,1)} %pad_maximum_fusion.1, s32[1024]{0:T(1024)S(1)} %pad_clamp_fusion), kind=kCustom, calls=%fused_computation.1 | custom fusion | bytes 23593600 | tf_op jit(solution)/shard_map/gather | solution.py:59
  73.4 0.0 copy-done.5
  73.4 10.4 %multiply_convert_fusion = (bf16[20,96,384]{2,1,0:T(8,128)(2,1)S(1)}, f32[20,96,384]{2,1,0:T(8,128)}) fusion(f32[20,96]{1,0:T(8,128)S(1)} %copy-done.4, f32[20,96,384]{2,1,0:T(8,128)} %get-tuple-element.25, bf16[20,96,384]{2,1,0:T(8,128)(2,1)} %param.9, bf16[20,96,384]{2,1,0:T(8,128)(2,1)} %copy-done.1, f32[20,96]{1,0:T(8,128)S(1)} %copy-done.5, ...), kind=kOutput, calls=%fused_computation.12 | convolution fusion | flops 1142784000 | bytes 25082880 | tf_op jit(solution)/shard_map/bik,bkr->bir/dot_general | solution.py:60
  83.8 0.0 copy-start.2
  83.8 0.1 fusion.8
  83.8 0.1 collective-permute-start.6
  83.9 3.5 %collective-permute-start.7 = (bf16[4,96,384]{2,1,0:T(8,128)(2,1)S(1)}, bf16[4,96,384]{2,1,0:T(8,128)(2,1)S(1)}, u32[]{:S(2)}, u32[]{:S(2)}) collective-permute-start(bf16[4,96,384]{2,1,0:T(8,128)(2,1)S(1)} %get-tuple-element.3), channel_id=1, source_target_pairs={{0,13},{1,0},{4,1},{5,4},{8,5},{9,8},{12,9},{13,12},{2,15},{3,2},{... | collective-permute-start | bytes 884744 | tf_op jit(solution)/shard_map/ppermute | solution.py:33
  87.4 6.7 %collective-permute-done.6 = bf16[4,96,384]{2,1,0:T(8,128)(2,1)S(1)} collective-permute-done((bf16[4,96,384]{2,1,0:T(8,128)(2,1)S(1)}, bf16[4,96,384]{2,1,0:T(8,128)(2,1)S(1)}, u32[]{:S(2)}, u32[]{:S(2)}) %collective-permute-start.6) | collective-permute-done | bytes 294944 | tf_op jit(solution)/shard_map/ppermute | solution.py:33
  94.1 0.0 collective-permute-done.7
  94.1 0.0 copy-done.2
  94.1 1.6 %pad_maximum_fusion.2 = bf16[28,96,384]{2,1,0:T(8,128)(2,1)} fusion(bf16[4,96,384]{2,1,0:T(8,128)(2,1)S(1)} %collective-permute-done.7, bf16[20,96,384]{2,1,0:T(8,128)(2,1)S(1)} %get-tuple-element.26, bf16[4,96,384]{2,1,0:T(8,128)(2,1)S(1)} %collective-permute-done.6), kind=kLoop, calls=%fused_computation.16 | loop fusion | flops 2064384 | bytes 4128768 | tf_op jit(solution)/shard_map/concatenate | solution.py:58
  95.8 10.3 %gather_fusion.2 = bf16[160,96,384]{2,1,0:T(8,128)(2,1)} fusion(bf16[28,96,384]{2,1,0:T(8,128)(2,1)} %pad_maximum_fusion.2, s32[1024]{0:T(1024)S(1)} %pad_clamp_fusion), kind=kCustom, calls=%fused_computation.2 | custom fusion | bytes 23593600 | tf_op jit(solution)/shard_map/gather | solution.py:59
  106.0 0.0 copy-done.7
  106.0 11.8 %fusion.5 = (f32[20,96,384]{2,1,0:T(8,128)}, f32[20,96,384]{2,1,0:T(8,128)}) fusion(f32[20,96,384]{2,1,0:T(8,128)} %get-tuple-element.27, f32[20,96,384]{2,1,0:T(8,128)} %get-tuple-element.25, bf16[20,96,384]{2,1,0:T(8,128)(2,1)} %param.9, bf16[20,96,384]{2,1,0:T(8,128)(2,1)} %copy-done.2, f32[20,96]{1,0:T(8,128)S(1)} %copy-done.7, ...), kind=kOutput, calls=%fused_computation.18 | convolution fusion | flops 1138360320 | bytes 29498880 | tf_op jit(solution)/shard_map/bik,bkr->bir/dot_general | solution.py:60
  (4 shorter events, 0.0 us)
Async XLA Ops:
  0.6 42.7 %copy-start = (bf16[20,96,768]{2,1,0:T(8,128)(2,1)S(1)}, bf16[20,96,768]{2,1,0:T(8,128)(2,1)}, u32[]{:S(2)}) copy-start(bf16[20,96,768]{2,1,0:T(8,128)(2,1)} %param.10) | copy-start | bytes 8847364
  0.6 12.4 %copy-start.8 = (s32[3,20]{1,0:T(4,128)S(1)}, s32[3,20]{1,0:T(4,128)}, u32[]{:S(2)}) copy-start(s32[3,20]{1,0:T(4,128)} %param.14) | copy-start | bytes 724
  2.1 14.9 %collective-permute-start.8 = (f32[1,20,48]{2,1,0:T(8,128)}, f32[1,20,48]{2,1,0:T(8,128)}, u32[]{:S(2)}, u32[]{:S(2)}) collective-permute-start(f32[1,20,48]{2,1,0:T(8,128)} %slice.47), channel_id=1, source_target_pairs={{0,2},{2,0},{1,3},{3,1},{4,6},{6,4},{5,7},{7,5},{8,10},{10,8},{9,1... | collective-permute-start | bytes 11528 | tf_op jit(solution)/shard_map/ppermute | solution.py:20
  7.5 1.1 copy-start.3
  9.5 20.7 %collective-permute-start = (bf16[4,96,384]{2,1,0:T(8,128)(2,1)}, bf16[4,96,384]{2,1,0:T(8,128)(2,1)S(1)}, u32[]{:S(2)}, u32[]{:S(2)}) collective-permute-start(bf16[4,96,384]{2,1,0:T(8,128)(2,1)} %get-tuple-element.6), channel_id=1, source_target_pairs={{0,1},{1,4},{4,5},{5,8},{8,9},{9,12},{12,13},{13,0},{2,3},{3,6},{6... | collective-permute-start | bytes 884744 | tf_op jit(solution)/shard_map/ppermute | solution.py:33
  9.5 20.7 %collective-permute-start.1 = (bf16[4,96,384]{2,1,0:T(8,128)(2,1)}, bf16[4,96,384]{2,1,0:T(8,128)(2,1)S(1)}, u32[]{:S(2)}, u32[]{:S(2)}) collective-permute-start(bf16[4,96,384]{2,1,0:T(8,128)(2,1)} %get-tuple-element.7), channel_id=1, source_target_pairs={{0,13},{1,0},{4,1},{5,4},{8,5},{9,8},{12,9},{13,12},{2,15},{3,2},{... | collective-permute-start | bytes 884744 | tf_op jit(solution)/shard_map/ppermute | solution.py:33
  18.4 4.0 %collective-permute-start.2 = (f32[1,20,48]{2,1,0:T(8,128)}, f32[1,20,48]{2,1,0:T(8,128)}, u32[]{:S(2)}, u32[]{:S(2)}) collective-permute-start(f32[1,20,48]{2,1,0:T(8,128)} %get-tuple-element.14), channel_id=1, source_target_pairs={{0,2},{2,0},{1,3},{3,1},{4,6},{6,4},{5,7},{7,5},{8,10},{10,8},{9,1... | collective-permute-start | bytes 11528 | tf_op jit(solution)/shard_map/ppermute | solution.py:20
  18.4 4.1 %collective-permute-start.5 = (f32[1,20,48]{2,1,0:T(8,128)}, f32[1,20,48]{2,1,0:T(8,128)}, u32[]{:S(2)}, u32[]{:S(2)}) collective-permute-start(f32[1,20,48]{2,1,0:T(8,128)} %get-tuple-element.15), channel_id=1, source_target_pairs={{0,2},{2,0},{1,3},{3,1},{4,6},{6,4},{5,7},{7,5},{8,10},{10,8},{9,1... | collective-permute-start | bytes 11528 | tf_op jit(solution)/shard_map/ppermute | solution.py:20
  33.1 10.3 %copy-start.4 = (f32[20,96]{1,0:T(8,128)S(1)}, f32[20,96]{1,0:T(8,128)}, u32[]{:S(2)}) copy-start(f32[20,96]{1,0:T(8,128)} %param.12) | copy-start | bytes 23044
  33.1 10.3 %copy-start.6 = (f32[20,96]{1,0:T(8,128)S(1)}, f32[20,96]{1,0:T(8,128)}, u32[]{:S(2)}) copy-start(f32[20,96]{1,0:T(8,128)} %get-tuple-element.19) | copy-start | bytes 23044
  50.9 10.6 %copy-start.1 = (bf16[20,96,384]{2,1,0:T(8,128)(2,1)}, bf16[20,96,384]{2,1,0:T(8,128)(2,1)S(1)}, u32[]{:S(2)}) copy-start(bf16[20,96,384]{2,1,0:T(8,128)(2,1)S(1)} %get-tuple-element.24) | copy-start | bytes 4423684
  51.0 10.5 %collective-permute-start.3 = (bf16[4,96,384]{2,1,0:T(8,128)(2,1)S(1)}, bf16[4,96,384]{2,1,0:T(8,128)(2,1)S(1)}, u32[]{:S(2)}, u32[]{:S(2)}) collective-permute-start(bf16[4,96,384]{2,1,0:T(8,128)(2,1)S(1)} %get-tuple-element.4), channel_id=1, source_target_pairs={{0,1},{1,4},{4,5},{5,8},{8,9},{9,12},{12,13},{13,0},{2,3},{3,6},{6... | collective-permute-start | bytes 884744 | tf_op jit(solution)/shard_map/ppermute | solution.py:33
  51.1 10.4 %collective-permute-start.4 = (bf16[4,96,384]{2,1,0:T(8,128)(2,1)S(1)}, bf16[4,96,384]{2,1,0:T(8,128)(2,1)S(1)}, u32[]{:S(2)}, u32[]{:S(2)}) collective-permute-start(bf16[4,96,384]{2,1,0:T(8,128)(2,1)S(1)} %get-tuple-element.5), channel_id=1, source_target_pairs={{0,13},{1,0},{4,1},{5,4},{8,5},{9,8},{12,9},{13,12},{2,15},{3,2},{... | collective-permute-start | bytes 884744 | tf_op jit(solution)/shard_map/ppermute | solution.py:33
  63.1 10.3 %copy-start.5 = (f32[20,96]{1,0:T(8,128)S(1)}, f32[20,96]{1,0:T(8,128)}, u32[]{:S(2)}) copy-start(f32[20,96]{1,0:T(8,128)} %get-tuple-element.20) | copy-start | bytes 23044
  83.8 10.3 %copy-start.2 = (bf16[20,96,384]{2,1,0:T(8,128)(2,1)}, bf16[20,96,384]{2,1,0:T(8,128)(2,1)S(1)}, u32[]{:S(2)}) copy-start(bf16[20,96,384]{2,1,0:T(8,128)(2,1)S(1)} %get-tuple-element.26) | copy-start | bytes 4423684
  83.8 10.3 %collective-permute-start.6 = (bf16[4,96,384]{2,1,0:T(8,128)(2,1)S(1)}, bf16[4,96,384]{2,1,0:T(8,128)(2,1)S(1)}, u32[]{:S(2)}, u32[]{:S(2)}) collective-permute-start(bf16[4,96,384]{2,1,0:T(8,128)(2,1)S(1)} %get-tuple-element.2), channel_id=1, source_target_pairs={{0,1},{1,4},{4,5},{5,8},{8,9},{9,12},{12,13},{13,0},{2,3},{3,6},{6... | collective-permute-start | bytes 884744 | tf_op jit(solution)/shard_map/ppermute | solution.py:33
  83.9 10.2 %collective-permute-start.7 = (bf16[4,96,384]{2,1,0:T(8,128)(2,1)S(1)}, bf16[4,96,384]{2,1,0:T(8,128)(2,1)S(1)}, u32[]{:S(2)}, u32[]{:S(2)}) collective-permute-start(bf16[4,96,384]{2,1,0:T(8,128)(2,1)S(1)} %get-tuple-element.3), channel_id=1, source_target_pairs={{0,13},{1,0},{4,1},{5,4},{8,5},{9,8},{12,9},{13,12},{2,15},{3,2},{... | collective-permute-start | bytes 884744 | tf_op jit(solution)/shard_map/ppermute | solution.py:33
  95.8 10.3 %copy-start.7 = (f32[20,96]{1,0:T(8,128)S(1)}, f32[20,96]{1,0:T(8,128)}, u32[]{:S(2)}) copy-start(f32[20,96]{1,0:T(8,128)} %get-tuple-element.18) | copy-start | bytes 23044
